TPU v7x, 256 devices: a whole 4x4x8 slice. The times are simulated.
256 devices in a mesh: rows: 64 (over z_lo, y, x, core), cols: 4 (over z_hi).
Axes of the slice: x: 4, y: 4, z: 8 (z_hi: 4, z_lo: 2; z = z_hi * 2 + z_lo), core: 2. Of those that a mesh axis runs over, the one named last changes fastest.
Arguments:
- design: bfloat16 [256, 1048576], P(None, 'rows'), may hold values from -0.28125 to 0.28125
- targets: bfloat16 [128, 1048576], P('cols', 'rows'), may hold values from -8 to 8
- flip_bits: int32 [2, 1048576], P(None, 'rows'), may hold values from 0 to 1
- listed: int32 [2, 32768], P(None, 'rows'), may hold values from 0 to 16383
- block_order: int32 [2, 64, 16], P(None, 'rows'), may hold values from 0 to 15, each once within a row
Outputs:
- solution: float32 [256, 128], P(None, 'cols')
- residual: float32 [128, 1048576], P('cols', 'rows')
Inputs may be any that keep to these rules, and one draw needn't show every extreme that they name: A group's listed rows are its own rows, counted from its first row; repeats may occur. `block_order`: for each step and group the 16 entries are a permutation.
All inputs are finite; a program needn't handle non-finite values.
Results may differ from a plain program's by a relative error of at most 0.017.
Values sent between devices are 32-bit elements; how exact they have to be, the bound alone decides.
A program may use at most 64 MiB of HBM per device.

v0:
```python
import math
import jax
import jax.numpy as jnp
from jax import lax
from jax.sharding import PartitionSpec as P


def on_device(design, targets, flip_bits, listed, block_order):
    unknowns, rows_here = design.shape
    steps_count = flip_bits.shape[0]
    blocks_count = block_order.shape[2]
    block_len = rows_here // blocks_count
    pick_count = listed.shape[1]
    col_share = unknowns // lax.axis_size("cols")
    inv_root = 1.0 / math.sqrt(block_len)
    keep_scale = math.sqrt(rows_here / pick_count)
    own_rows = lax.dynamic_slice_in_dim(design, lax.axis_index("cols") * col_share, col_share, 0)
    positions = jnp.arange(block_len, dtype=jnp.int32)[:, None]
    block_ids = jnp.arange(blocks_count, dtype=jnp.int32)[:, None]
    unit_eye = jnp.eye(unknowns, dtype=jnp.float32)

    def misfit_of(solution):
        product = lax.dot_general(
            solution.astype(jnp.bfloat16),
            design,
            (((0,), (0,)), ((), ())),
            preferred_element_type=jnp.float32,
        )
        return product - targets.astype(jnp.float32)

    solution = jnp.zeros((unknowns, targets.shape[0]), jnp.float32)
    for step_index in range(steps_count):
        sign_rows = (
            (2 * flip_bits[step_index] - 1).astype(jnp.bfloat16).reshape(blocks_count, block_len)
        )
        chosen = listed[step_index]
        order_now = block_order[step_index, 0]
        target_block = chosen // block_len
        within = chosen % block_len
        source = jnp.sum(
            jnp.where(target_block[None, :] == block_ids, order_now[:, None], 0), axis=0
        )
        parity = jnp.zeros((block_len, pick_count), jnp.int32)
        for bit_index in range(block_len.bit_length() - 1):
            parity = parity ^ positions >> bit_index & 1 & (within[None, :] >> bit_index & 1)
        walsh = (1 - 2 * parity).astype(jnp.bfloat16)
        placed = (source[None, :] == block_ids).astype(jnp.bfloat16)
        table = (placed[:, None, :] * sign_rows[:, :, None] * walsh[None, :, :]).reshape(
            rows_here, pick_count
        )
        mixed_rows = (
            jnp.dot(own_rows, table, preferred_element_type=jnp.float32) * inv_root
        ).astype(jnp.bfloat16)
        summed = lax.psum((mixed_rows.astype(jnp.float32) * keep_scale)[None], "rows")
        whole_sketch = lax.all_gather(summed, "cols", axis=1, tiled=True)
        gram_stack = jnp.einsum(
            "npm,nqm->npq", whole_sketch, whole_sketch, precision=lax.Precision.HIGHEST
        )
        shift = jnp.trace(gram_stack, axis1=1, axis2=2) / unknowns
        gram_now = (gram_stack + shift[:, None, None] * unit_eye[None])[0]
        if step_index == 0:
            misfit_half = -targets
        else:
            misfit_half = misfit_of(solution).astype(jnp.bfloat16)
        local_grad = lax.dot_general(
            design, misfit_half, (((1,), (1,)), ((), ())), preferred_element_type=jnp.float32
        )
        gradient = lax.psum(local_grad, "rows")
        factor = jnp.linalg.cholesky(gram_now)
        solution = solution - jax.scipy.linalg.cho_solve((factor, True), gradient)
    return (solution, misfit_of(solution))


def solution(mesh):
    return jax.shard_map(
        on_device,
        mesh=mesh,
        in_specs=(
            P(None, "rows"),
            P("cols", "rows"),
            P(None, "rows"),
            P(None, "rows"),
            P(None, "rows", None),
        ),
        out_specs=(P(None, "cols"), P("cols", "rows")),
        check_vma=False,
    )
```

profile of v0, /device:TPU:32, one launch (start us, length us, event | category | flops | bytes accessed | tf_op | source)
XLA Modules:
  0.0 1007.5 jit_solution(7467058959739676185)
XLA Ops:
  7.3 0.8 and_select_fusion.3
  8.9 1.4 convert_reduce_fusion.1
  10.4 2.0 subtract_convert_fusion.1
  12.4 2.8 bitcast_multiply_fusion.2
  15.2 3.7 fusion.32
  18.9 2.0 subtract_convert_fusion
  20.9 2.8 bitcast_multiply_fusion
  23.7 3.7 fusion.20
  27.4 6.0 fusion.35
  33.4 279.1 %psum.29 = f32[256,32]{0,1:T(8,128)S(1)} all-reduce(f32[256,32]{0,1:T(8,128)S(1)} %fusion.35), channel_id=1, replica_groups=mesh['rows'=64,'cols'=4] {'rows'}, use_global_device_ids=true, to_apply=%region_7.9 | all-reduce | flops 8192 | bytes 65536 | tf_op jit(solution)/shard_map/psum | solution.py:68
  312.5 231.7 %all-reduce.4.cloned.1.call-done = (f32[1,64,512]{2,1,0:T(8,128)}, f32[1,64,512]{2,1,0:T(8,128)}) async-done(((f32[1,64,512]{2,1,0:T(8,128)}, f32[1,64,512]{2,1,0:T(8,128)}), (f32[1,64,512]{2,1,0:T(8,128)}, f32[1,64,512]{2,1,0:T(8,128)})) %all-reduce.4.cloned.1.call-update) | async-done | bytes 262160 | tf_op jit(solution)/shard_map/psum | solution.py:54
  544.2 18.6 %all_gather.6 = f32[1,256,512]{2,1,0:T(8,128)S(1)} all-gather(f32[1,64,512]{2,1,0:T(8,128)} %get-tuple-element.39), channel_id=1, replica_groups=mesh['rows'=64,'cols'=4] {'cols'}, dimensions={1}, use_global_device_ids=true | all-gather | bytes 655360 | tf_op jit(solution)/shard_map/all_gather | solution.py:55
  562.8 1.2 select_reduce_fusion.1
  564.9 11.7 %cholesky.130 = f32[128,128]{1,0:T(8,128)S(1)} custom-call(f32[128,128]{1,0:T(8,128)S(1)} %cholesky.194), custom_call_target="Cholesky" | custom-call | tf_op jit(solution)/shard_map/jit(cholesky)/cholesky | solution.py:69
  576.7 9.8 custom-call.15
  587.0 11.7 %cholesky.147 = f32[128,128]{1,0:T(8,128)S(1)} custom-call(f32[128,128]{1,0:T(8,128)S(1)} %convolution_subtract_fusion.3), custom_call_target="Cholesky" | custom-call | tf_op jit(solution)/shard_map/jit(cholesky)/cholesky | solution.py:69
  601.3 4.0 while.4
  602.1 1.3 bitcast_dynamic-update-slice_fusion.4
  604.1 1.3 bitcast_dynamic-update-slice_fusion.4
  605.4 19.7 %custom-call.16 = f32[2,128,128]{1,2,0:T(8,128)S(1)} custom-call(f32[2,128,128]{2,1,0:T(8,128)S(1)} %get-tuple-element.18), custom_call_target="InvertDiagBlocksLowerTriangular" | custom-call | tf_op jit(solution)/shard_map/jit(_cho_solve)/triangular_solve | solution.py:70
  626.4 9.9 convolution_bitcast_fusion
  636.3 277.7 %psum.31 = f32[256,32]{0,1:T(8,128)S(1)} all-reduce(f32[256,32]{0,1:T(8,128)S(1)} %convolution_bitcast_fusion), channel_id=1, replica_groups=mesh['rows'=64,'cols'=4] {'rows'}, use_global_device_ids=true, to_apply=%region_11.14 | all-reduce | flops 8192 | bytes 65536 | tf_op jit(solution)/shard_map/psum | solution.py:68
  914.0 15.9 %all_gather.7 = f32[1,256,512]{2,1,0:T(8,128)S(1)} all-gather(f32[1,64,512]{2,1,0:T(8,128)S(1)} %copy-done.2), channel_id=1, replica_groups=mesh['rows'=64,'cols'=4] {'cols'}, dimensions={1}, use_global_device_ids=true | all-gather | bytes 655360 | tf_op jit(solution)/shard_map/all_gather | solution.py:55
  929.8 1.2 select_reduce_fusion
  931.9 11.7 %cholesky.164 = f32[128,128]{1,0:T(8,128)S(1)} custom-call(f32[128,128]{1,0:T(8,128)S(1)} %cholesky.197), custom_call_target="Cholesky" | custom-call | tf_op jit(solution)/shard_map/jit(cholesky)/cholesky | solution.py:69
  943.7 9.8 custom-call.17
  954.0 11.7 %cholesky.181 = f32[128,128]{1,0:T(8,128)S(1)} custom-call(f32[128,128]{1,0:T(8,128)S(1)} %convolution_subtract_fusion.2), custom_call_target="Cholesky" | custom-call | tf_op jit(solution)/shard_map/jit(cholesky)/cholesky | solution.py:69
  968.5 4.4 while.5
  969.4 1.4 bitcast_dynamic-update-slice_fusion.5
  971.4 1.4 bitcast_dynamic-update-slice_fusion.5
  972.9 19.7 %custom-call.18 = f32[2,128,128]{1,2,0:T(8,128)S(1)} custom-call(f32[2,128,128]{2,1,0:T(8,128)S(1)} %get-tuple-element.19), custom_call_target="InvertDiagBlocksLowerTriangular" | custom-call | tf_op jit(solution)/shard_map/jit(_cho_solve)/triangular_solve | solution.py:70
  993.9 6.3 convolution_subtract_fusion
  (74 shorter events, 10.2 us)
Async XLA Ops:
  7.2 537.0 %all-reduce.4.cloned.1.call-start = ((), (), s32[]{:S(2)}) async-start(), calls=%async_computation | async-start | bytes 524288 | tf_op jit(solution)/shard_map/psum | solution.py:54
  10.3 4.9 slice-start
  12.4 2.8 slice-start.1
  23.7 3.7 copy-start
  626.4 287.6 %copy-start.2 = (f32[1,64,512]{2,1,0:T(8,128)S(1)}, f32[1,64,512]{2,1,0:T(8,128)}, u32[]{:S(2)}) copy-start(f32[1,64,512]{2,1,0:T(8,128)} %get-tuple-element.38) | copy-start | bytes 393220
  993.9 6.3 copy-start.1
Sparse Core Ops, SparseCore 0:
  27.5 516.6 all-reduce.3
where the time goes:
time: 1010 us
  blocking collectives  591 us (59%)
  waiting for transfers between devices  232 us (23%)
  other arithmetic  121 us (12%)
  matrix products  35.3 us (3%)
  between operations  18.9 us (2%)
    psum x2, blocking collectives, on_device(): gradient = lax.psum(local_grad, 'rows')  557 us
    psum x1, waiting for transfers between devices, on_device(): lax.psum((mixed_rows.astype(jnp.float32) * keep_scale)[None], 'rows')  232 us
    another operation x14, other arithmetic, on_device(): factor = jnp.linalg.cholesky(gram_now)  69.2 us
    another operation x5, other arithmetic, on_device(): solution = solution - jax.scipy.linalg.cho_solve((factor, True), gradient)  39.4 us
    all_gather x2, blocking collectives, on_device(): whole_sketch = lax.all_gather(summed, 'cols', axis=1, tiled=True)  34.5 us
  transfers between devices with their start and end apart: 1, of which 1 were waited for; matrix products, arithmetic and copies ran while one was open for 1% of the time, Pallas kernels for 0%

commit v1 on v0

--- a/solution.py
+++ b/solution.py
@@ -51,7 +51,9 @@
         mixed_rows = (
             jnp.dot(own_rows, table, preferred_element_type=jnp.float32) * inv_root
         ).astype(jnp.bfloat16)
-        summed = lax.psum((mixed_rows.astype(jnp.float32) * keep_scale)[None], "rows")
+        summed = jnp.sum(
+            lax.all_gather((mixed_rows.astype(jnp.float32) * keep_scale)[None], "rows"), axis=0
+        )
         whole_sketch = lax.all_gather(summed, "cols", axis=1, tiled=True)
         gram_stack = jnp.einsum(
             "npm,nqm->npq", whole_sketch, whole_sketch, precision=lax.Precision.HIGHEST

time: 1010 us -> 792 us (0.78)
  waiting for transfers between devices: 232 us -> 0.04 us
    psum x1 -> x0, waiting for transfers between devices: 232 us -> none  [on_device(): lax.psum((mixed_rows.astype(jnp.float32) * keep_scale)[None], 'rows')]
  transfers between devices with their start and end apart: 1 -> 2, of which waited for: 1 -> 0; matrix products, arithmetic and copies ran while one was open for 1% -> 12% of each run, Pallas kernels for 0% -> 0%
where the time goes in v1:
time: 792 us; the launch traced here: 784 us
  blocking collectives  588 us (74%)
  other arithmetic  129 us (16%)
  matrix products  38.5 us (5%)
  between operations  18.6 us (2%)
  local copies, waits for them, and re-layouts  8.84 us (1%)
    psum x2, blocking collectives, on_device(): gradient = lax.psum(local_grad, 'rows')  554 us
    another operation x14, other arithmetic, on_device(): factor = jnp.linalg.cholesky(gram_now)  69.2 us
    another operation x5, other arithmetic, on_device(): solution = solution - jax.scipy.linalg.cho_solve((factor, True), gradient)  39.4 us
    all_gather x2, blocking collectives, on_device(): whole_sketch = lax.all_gather(summed, 'cols', axis=1, tiled=True)  34.3 us
  transfers between devices with their start and end apart: 2, of which 0 were waited for; matrix products, arithmetic and copies ran while one was open for 12% of the time, Pallas kernels for 0%

profile of v1, /device:TPU:32, one launch (start us, length us, event | category | flops | bytes accessed | tf_op | source)
XLA Modules:
  0.0 783.9 jit_solution(5178904618849144703)
XLA Ops:
  8.9 1.4 convert_reduce_fusion.1
  10.3 2.0 subtract_convert_fusion.1
  12.3 2.8 bitcast_multiply_fusion.2
  15.1 5.2 fusion.26
  20.5 2.0 subtract_convert_fusion
  22.5 2.8 bitcast_multiply_fusion
  25.3 5.3 fusion.17
  30.7 6.0 fusion.29
  36.7 279.2 %psum.14 = f32[256,32]{0,1:T(8,128)S(1)} all-reduce(f32[256,32]{0,1:T(8,128)S(1)} %fusion.29), channel_id=1, replica_groups=mesh['rows'=64,'cols'=4] {'rows'}, use_global_device_ids=true, to_apply=%region_7.9 | all-reduce | flops 8192 | bytes 65536 | tf_op jit(solution)/shard_map/psum | solution.py:70
  315.9 4.1 reduce.14
  320.0 19.4 %all-gather.1 = f32[256,512]{1,0:T(8,128)S(1)} all-gather(f32[64,512]{1,0:T(8,128)S(1)} %reduce.14), channel_id=3, replica_groups=mesh['rows'=64,'cols'=4] {'cols'}, dimensions={0}, use_global_device_ids=true | all-gather | bytes 655360 | tf_op jit(solution)/shard_map/all_gather | solution.py:57
  339.3 1.2 select_reduce_fusion.1
  341.3 11.7 %cholesky.130 = f32[128,128]{1,0:T(8,128)S(1)} custom-call(f32[128,128]{1,0:T(8,128)S(1)} %cholesky.194), custom_call_target="Cholesky" | custom-call | tf_op jit(solution)/shard_map/jit(cholesky)/cholesky | solution.py:71
  353.1 9.8 %custom-call.15 = f32[1,128,128]{1,2,0:T(8,128)S(1)} custom-call(f32[1,128,128]{2,1,0:T(8,128)S(1)} %get-tuple-element.53), custom_call_target="InvertDiagBlocksLowerTriangular" | custom-call | tf_op jit(solution)/shard_map/jit(cholesky)/cholesky | solution.py:71
  363.4 11.7 %cholesky.147 = f32[128,128]{1,0:T(8,128)S(1)} custom-call(f32[128,128]{1,0:T(8,128)S(1)} %convolution_subtract_fusion.3), custom_call_target="Cholesky" | custom-call | tf_op jit(solution)/shard_map/jit(cholesky)/cholesky | solution.py:71
  377.7 3.9 while.4
  378.5 1.3 bitcast_dynamic-update-slice_fusion.4
  380.4 1.3 bitcast_dynamic-update-slice_fusion.4
  381.7 19.7 %custom-call.16 = f32[2,128,128]{1,2,0:T(8,128)S(1)} custom-call(f32[2,128,128]{2,1,0:T(8,128)S(1)} %get-tuple-element.18), custom_call_target="InvertDiagBlocksLowerTriangular" | custom-call | tf_op jit(solution)/shard_map/jit(_cho_solve)/triangular_solve | solution.py:72
  402.7 9.8 %convolution_bitcast_fusion = f32[256,32]{0,1:T(8,128)S(1)} fusion(bf16[256,16384]{1,0:T(8,128)(2,1)} %param.8, bf16[32,16384]{1,0:T(8,128)(2,1)S(1)} %copy-done, f32[128,32]{0,1:T(8,128)S(1)} %fusion.41, f32[128,32]{0,1:T(8,128)S(1)} %fusion.39), kind=kOutput, calls=%fused_computation.27 | convolution fusion | flops 538468352 | bytes 9502720 | tf_op jit(solution)/shard_map/dot_general | solution.py:67
  412.5 274.9 %psum.15 = f32[256,32]{0,1:T(8,128)S(1)} all-reduce(f32[256,32]{0,1:T(8,128)S(1)} %convolution_bitcast_fusion), channel_id=1, replica_groups=mesh['rows'=64,'cols'=4] {'rows'}, use_global_device_ids=true, to_apply=%region_11.14 | all-reduce | flops 8192 | bytes 65536 | tf_op jit(solution)/shard_map/psum | solution.py:70
  687.5 4.1 reduce.15
  691.6 14.9 %all-gather.3 = f32[256,512]{1,0:T(8,128)S(1)} all-gather(f32[64,512]{1,0:T(8,128)S(1)} %reduce.15), channel_id=5, replica_groups=mesh['rows'=64,'cols'=4] {'cols'}, dimensions={0}, use_global_device_ids=true | all-gather | bytes 655360 | tf_op jit(solution)/shard_map/all_gather | solution.py:57
  706.5 1.2 select_reduce_fusion
  708.6 11.7 %cholesky.164 = f32[128,128]{1,0:T(8,128)S(1)} custom-call(f32[128,128]{1,0:T(8,128)S(1)} %cholesky.197), custom_call_target="Cholesky" | custom-call | tf_op jit(solution)/shard_map/jit(cholesky)/cholesky | solution.py:71
  720.3 9.8 %custom-call.17 = f32[1,128,128]{1,2,0:T(8,128)S(1)} custom-call(f32[1,128,128]{2,1,0:T(8,128)S(1)} %get-tuple-element.57), custom_call_target="InvertDiagBlocksLowerTriangular" | custom-call | tf_op jit(solution)/shard_map/jit(cholesky)/cholesky | solution.py:71
  730.6 11.7 %cholesky.181 = f32[128,128]{1,0:T(8,128)S(1)} custom-call(f32[128,128]{1,0:T(8,128)S(1)} %convolution_subtract_fusion.2), custom_call_target="Cholesky" | custom-call | tf_op jit(solution)/shard_map/jit(cholesky)/cholesky | solution.py:71
  745.1 4.4 while.5
  746.0 1.4 bitcast_dynamic-update-slice_fusion.5
  748.1 1.4 bitcast_dynamic-update-slice_fusion.5
  749.5 19.7 %custom-call.18 = f32[2,128,128]{1,2,0:T(8,128)S(1)} custom-call(f32[2,128,128]{2,1,0:T(8,128)S(1)} %get-tuple-element.19), custom_call_target="InvertDiagBlocksLowerTriangular" | custom-call | tf_op jit(solution)/shard_map/jit(_cho_solve)/triangular_solve | solution.py:72
  770.6 6.3 convolution_subtract_fusion
  (72 shorter events, 11.0 us)
Async XLA Ops:
  7.2 308.7 %all-gather.7.cloned.1.call-start = ((), (), s32[]{:S(2)}) async-start(), calls=%async_computation | async-start | bytes 8519680 | tf_op jit(solution)/shard_map/all_gather | solution.py:55
  20.4 667.1 %all-gather.9.cloned.1.call-start = ((), (), s32[]{:S(2)}) async-start(), calls=%async_computation.1 | async-start | bytes 8519680 | tf_op jit(solution)/shard_map/all_gather | solution.py:55
  25.3 5.4 copy-start
  770.6 6.3 copy-start.1
Sparse Core Ops, SparseCore 0:
  20.5 114.7 all-gather.6
  137.7 111.8 all-gather.8

commit v2 on v0

--- a/solution.py
+++ b/solution.py
@@ -65,7 +65,7 @@
         local_grad = lax.dot_general(
             design, misfit_half, (((1,), (1,)), ((), ())), preferred_element_type=jnp.float32
         )
-        gradient = lax.psum(local_grad, "rows")
+        gradient = jnp.sum(lax.all_gather(local_grad, "rows"), axis=0)
         factor = jnp.linalg.cholesky(gram_now)
         solution = solution - jax.scipy.linalg.cho_solve((factor, True), gradient)
     return (solution, misfit_of(solution))

time: 1010 us -> 799 us (0.79)
  blocking collectives: 591 us -> 37.6 us
  waiting for transfers between devices: 232 us -> 563 us
    psum x2 -> x0, blocking collectives: 557 us -> none  [on_device(): gradient = lax.psum(local_grad, 'rows')]
    psum x1, waiting for transfers between devices: 232 us -> 510 us  [on_device(): lax.psum((mixed_rows.astype(jnp.float32) * keep_scale)[None], 'rows')]
    all_gather x0 -> x2, waiting for transfers between devices: none -> 53 us  [on_device(): gradient = jnp.sum(lax.all_gather(local_grad, 'rows'), axis=0)]
  transfers between devices with their start and end apart: 1 -> 3, of which waited for: 1 -> 3; matrix products, arithmetic and copies ran while one was open for 1% -> 16% of each run, Pallas kernels for 0% -> 0%
where the time goes in v2:
time: 799 us; the launch traced here: 791 us
  waiting for transfers between devices  563 us (70%)
  other arithmetic  121 us (15%)
  blocking collectives  37.6 us (5%)
  matrix products  36.2 us (5%)
  between operations  18.4 us (2%)
  local copies, waits for them, and re-layouts  13.5 us (2%)
    psum x1, waiting for transfers between devices, on_device(): lax.psum((mixed_rows.astype(jnp.float32) * keep_scale)[None], 'rows')  510 us
    another operation x14, other arithmetic, on_device(): factor = jnp.linalg.cholesky(gram_now)  69.2 us
    all_gather x2, waiting for transfers between devices, on_device(): gradient = jnp.sum(lax.all_gather(local_grad, 'rows'), axis=0)  53 us
    another operation x5, other arithmetic, on_device(): solution = solution - jax.scipy.linalg.cho_solve((factor, True), gradient)  39.4 us
    all_gather x2, blocking collectives, on_device(): whole_sketch = lax.all_gather(summed, 'cols', axis=1, tiled=True)  37.6 us
    dot_general x2, matrix products, on_device(): lax.dot_general(design, misfit_half, (((1,), (1,)), ((), ())), preferred_...  17.1 us
  transfers between devices with their start and end apart: 3, of which 3 were waited for; matrix products, arithmetic and copies ran while one was open for 16% of the time, Pallas kernels for 0%

profile of v2, /device:TPU:32, one launch (start us, length us, event | category | flops | bytes accessed | tf_op | source)
XLA Modules:
  0.0 790.6 jit_solution(14491040255093824703)
XLA Ops:
  8.9 1.4 convert_reduce_fusion.1
  10.4 2.0 subtract_convert_fusion.1
  12.4 2.8 bitcast_multiply_fusion.2
  15.2 3.7 fusion.32
  18.9 2.0 subtract_convert_fusion
  20.9 2.8 bitcast_multiply_fusion
  23.7 3.7 fusion.20
  27.4 6.6 fusion.35
  34.1 510.1 %all-reduce.4.cloned.1.call-done = (f32[1,64,512]{2,1,0:T(8,128)}, f32[1,64,512]{2,1,0:T(8,128)}) async-done(((f32[1,64,512]{2,1,0:T(8,128)}, f32[1,64,512]{2,1,0:T(8,128)}), (f32[1,64,512]{2,1,0:T(8,128)}, f32[1,64,512]{2,1,0:T(8,128)})) %all-reduce.4.cloned.1.call-update) | async-done | bytes 262160 | tf_op jit(solution)/shard_map/psum | solution.py:54
  544.2 19.0 %all_gather.18 = f32[1,256,512]{2,1,0:T(8,128)S(1)} all-gather(f32[1,64,512]{2,1,0:T(8,128)} %get-tuple-element.39), channel_id=1, replica_groups=mesh['rows'=64,'cols'=4] {'cols'}, dimensions={1}, use_global_device_ids=true | all-gather | bytes 655360 | tf_op jit(solution)/shard_map/all_gather | solution.py:55
  563.1 1.2 select_reduce_fusion.1
  565.2 11.7 %cholesky.130 = f32[128,128]{1,0:T(8,128)S(1)} custom-call(f32[128,128]{1,0:T(8,128)S(1)} %cholesky.194), custom_call_target="Cholesky" | custom-call | tf_op jit(solution)/shard_map/jit(cholesky)/cholesky | solution.py:69
  577.0 9.8 %custom-call.15 = f32[1,128,128]{1,2,0:T(8,128)S(1)} custom-call(f32[1,128,128]{2,1,0:T(8,128)S(1)} %get-tuple-element.55), custom_call_target="InvertDiagBlocksLowerTriangular" | custom-call | tf_op jit(solution)/shard_map/jit(cholesky)/cholesky | solution.py:69
  587.3 11.7 %cholesky.147 = f32[128,128]{1,0:T(8,128)S(1)} custom-call(f32[128,128]{1,0:T(8,128)S(1)} %convolution_subtract_fusion.3), custom_call_target="Cholesky" | custom-call | tf_op jit(solution)/shard_map/jit(cholesky)/cholesky | solution.py:69
  601.8 4.2 while.4
  602.6 1.4 bitcast_dynamic-update-slice_fusion.4
  604.7 1.4 bitcast_dynamic-update-slice_fusion.4
  606.1 19.7 %custom-call.16 = f32[2,128,128]{1,2,0:T(8,128)S(1)} custom-call(f32[2,128,128]{2,1,0:T(8,128)S(1)} %get-tuple-element.18), custom_call_target="InvertDiagBlocksLowerTriangular" | custom-call | tf_op jit(solution)/shard_map/jit(_cho_solve)/triangular_solve | solution.py:70
  625.8 28.6 %all-gather.5.cloned.1.call-done = f32[16384,32]{0,1:T(8,128)} async-done(((f32[256,32]{0,1:T(8,128)}), f32[16384,32]{0,1:T(8,128)}) %all-gather.5.cloned.1.call-update) | async-done | bytes 2097168 | tf_op jit(solution)/shard_map/all_gather | solution.py:68
  654.3 2.2 copy.27
  657.9 10.5 %convolution_bitcast_fusion = f32[256,32]{0,1:T(8,128)} fusion(bf16[256,16384]{1,0:T(8,128)(2,1)} %param.8, bf16[32,16384]{1,0:T(8,128)(2,1)S(1)} %copy-done, f32[128,32]{0,1:T(8,128)S(1)} %fusion.51, f32[128,32]{0,1:T(8,128)S(1)} %fusion.49), kind=kOutput, calls=%fused_computation.31 | convolution fusion | flops 538468352 | bytes 9502720 | tf_op jit(solution)/shard_map/dot_general | solution.py:65
  668.5 18.7 %all_gather.21 = f32[1,256,512]{2,1,0:T(8,128)S(1)} all-gather(f32[1,64,512]{2,1,0:T(8,128)S(1)} %copy-done.2), channel_id=1, replica_groups=mesh['rows'=64,'cols'=4] {'cols'}, dimensions={1}, use_global_device_ids=true | all-gather | bytes 655360 | tf_op jit(solution)/shard_map/all_gather | solution.py:55
  689.2 11.7 %cholesky.164 = f32[128,128]{1,0:T(8,128)S(1)} custom-call(f32[128,128]{1,0:T(8,128)S(1)} %cholesky.197), custom_call_target="Cholesky" | custom-call | tf_op jit(solution)/shard_map/jit(cholesky)/cholesky | solution.py:69
  701.0 9.8 %custom-call.17 = f32[1,128,128]{1,2,0:T(8,128)S(1)} custom-call(f32[1,128,128]{2,1,0:T(8,128)S(1)} %get-tuple-element.59), custom_call_target="InvertDiagBlocksLowerTriangular" | custom-call | tf_op jit(solution)/shard_map/jit(cholesky)/cholesky | solution.py:69
  711.3 11.7 %cholesky.181 = f32[128,128]{1,0:T(8,128)S(1)} custom-call(f32[128,128]{1,0:T(8,128)S(1)} %convolution_subtract_fusion.2), custom_call_target="Cholesky" | custom-call | tf_op jit(solution)/shard_map/jit(cholesky)/cholesky | solution.py:69
  725.7 4.2 while.5
  726.5 1.4 bitcast_dynamic-update-slice_fusion.5
  728.5 1.4 bitcast_dynamic-update-slice_fusion.5
  729.9 19.7 %custom-call.18 = f32[2,128,128]{1,2,0:T(8,128)S(1)} custom-call(f32[2,128,128]{2,1,0:T(8,128)S(1)} %get-tuple-element.19), custom_call_target="InvertDiagBlocksLowerTriangular" | custom-call | tf_op jit(solution)/shard_map/jit(_cho_solve)/triangular_solve | solution.py:70
  749.6 24.4 %all-gather.7.cloned.1.call-done = f32[16384,32]{0,1:T(8,128)} async-done(((f32[256,32]{0,1:T(8,128)}), f32[16384,32]{0,1:T(8,128)}) %all-gather.7.cloned.1.call-update) | async-done | bytes 2097168 | tf_op jit(solution)/shard_map/all_gather | solution.py:68
  774.0 2.2 copy.28
  777.6 6.3 convolution_subtract_fusion
  (82 shorter events, 12.3 us)
Async XLA Ops:
  7.2 537.0 %all-reduce.4.cloned.1.call-start = ((), (), s32[]{:S(2)}) async-start(), calls=%async_computation.2 | async-start | bytes 524288 | tf_op jit(solution)/shard_map/psum | solution.py:54
  10.3 4.9 slice-start
  12.4 2.8 slice-start.1
  23.7 3.8 copy-start
  27.4 627.0 %all-gather.5.cloned.1.call-start = ((), (), s32[]{:S(2)}) async-start(), calls=%async_computation | async-start | bytes 2129920 | tf_op jit(solution)/shard_map/all_gather | solution.py:68
  34.0 739.9 %all-gather.7.cloned.1.call-start = ((), (), s32[]{:S(2)}) async-start(), calls=%async_computation.1 | async-start | bytes 2129920 | tf_op jit(solution)/shard_map/all_gather | solution.py:68
  657.9 10.5 %copy-start.2 = (f32[1,64,512]{2,1,0:T(8,128)S(1)}, f32[1,64,512]{2,1,0:T(8,128)}, u32[]{:S(2)}) copy-start(f32[1,64,512]{2,1,0:T(8,128)} %get-tuple-element.38) | copy-start | bytes 393220
  777.6 6.3 copy-start.1
Sparse Core Ops, SparseCore 0:
  27.5 516.6 all-reduce.3
  546.6 107.6 all-gather.4
  668.6 105.3 all-gather.6
